TPU v7x, 32 devices: a whole 2x2x4 slice. The times are simulated.
32 devices in a mesh: section: 2 (over core), ctx: 4 (over z), mp: 4 (over y, x).
Axes of the slice: x: 2, y: 2, z: 4, core: 2. Of those that a mesh axis runs over, the one named last changes fastest.
Arguments:
- frames: bfloat16 [2, 16, 128, 512], P('section', 'ctx'), may hold values from -6 to 6
- w_conv: bfloat16 [3, 512, 512], replicated, may hold values from -0.15625 to 0.15625
- w_lat: bfloat16 [512, 16], replicated, may hold values from -0.25 to 0.25
- dest: int32 [2, 512, 1], P(None, 'ctx'), may hold values from 0 to 3; in each aligned block of 128 rows (0 to 127, 128 to 255, ..., all dimensions but the last counted through in order) at most 48 rows name the same one
- pick: int32 [2, 512], P(None, 'ctx'), may hold values from 0 to 6
- w_embed: bfloat16 [64, 6144], replicated, may hold values from -0.75 to 0.75
- gain: float32 [6144], replicated, may hold values from 0.25 to 1.75
- w_qkv: bfloat16 [6144, 3, 4096], P(None, None, 'mp'), may hold values from -0.078125 to 0.078125
Outputs:
- attended: bfloat16 [2, 768, 4096], P('section', 'ctx', 'mp')
Inputs may be any that keep to these rules, and one draw needn't show every extreme that they name: `dest`: among the 128 rows of one frame block, at most 48 name the same context shard, and some frame block reaches 48.
All inputs are finite; a program needn't handle non-finite values.
Results may differ from a plain program's by a relative error of at most 0.0061.
Values may be sent and summed in bfloat16 or wider, within the bound.
A program may use at most 128 MiB of HBM per device.

v0:
```python
import jax
import jax.numpy as jnp
from jax import lax
from jax.sharding import PartitionSpec as P

HEAD = 128
GROUP = 4


def partner(block, axis, distance):
    count = lax.axis_size(axis)
    route = []
    for low in range(count):
        high = low | 1 << distance
        if high != low and high < count:
            route += [(low, high), (high, low)]
    return lax.ppermute(block, axis, route)


def encode(frame_block, w_conv, w_lat):
    frame_count = frame_block.shape[0]
    cells_here = frame_block.shape[1]
    channels = frame_block.shape[2]
    empty_frame = jnp.zeros_like(frame_block[:1])
    back_one = jnp.concatenate([empty_frame, frame_block[:-1]], axis=0)
    back_two = jnp.concatenate([empty_frame, empty_frame, frame_block[:-2]], axis=0)
    hidden = jnp.dot(
        frame_block.reshape(-1, channels), w_conv[0], preferred_element_type=jnp.float32
    )
    hidden = hidden + jnp.dot(
        back_one.reshape(-1, channels), w_conv[1], preferred_element_type=jnp.float32
    )
    hidden = hidden + jnp.dot(
        back_two.reshape(-1, channels), w_conv[2], preferred_element_type=jnp.float32
    )
    active = jax.nn.silu(hidden).astype(jnp.bfloat16)
    latent = jnp.dot(active, w_lat, preferred_element_type=jnp.float32).astype(jnp.bfloat16)
    return latent.reshape(frame_count, cells_here // 4, 4 * w_lat.shape[1])


def head_norm(values):
    return values * lax.rsqrt(jnp.mean(values * values, axis=-1, keepdims=True) + 1e-06)


def on_device(frames, w_conv, w_lat, dest, pick, w_embed, gain, w_qkv):
    frame_block = frames[0]
    patch_grid = encode(frame_block, w_conv, w_lat)
    patch_rows = patch_grid.reshape(-1, patch_grid.shape[-1])
    arrived = partner(patch_rows, "section", 0)
    shard_count = lax.axis_size("ctx")
    row_count = arrived.shape[0]
    source = 1 - lax.axis_index("section")
    targets = lax.dynamic_index_in_dim(dest[:, :, 0], source, 0, keepdims=False)
    choose = lax.dynamic_index_in_dim(pick, source, 0, keepdims=False)
    tier = (choose >= 4).astype(jnp.int32) + (choose >= 6).astype(jnp.int32)
    labels = targets // GROUP + shard_count // GROUP * tier + 1
    onehot = (targets[:, None] == jnp.arange(shard_count, dtype=jnp.int32)[None, :]).astype(
        jnp.int32
    )
    before = jnp.cumsum(onehot, axis=0, dtype=jnp.int32) - onehot
    within = jnp.sum(before * onehot, axis=1, dtype=jnp.int32)
    capacity = max(2, 3 * row_count // (2 * shard_count))
    position = targets * capacity + within
    outgoing = (
        jnp.zeros((shard_count * capacity, arrived.shape[1]), jnp.bfloat16)
        .at[position]
        .set(arrived)
    )
    outgoing = outgoing.reshape(shard_count, capacity, arrived.shape[1])
    out_labels = jnp.zeros((shard_count * capacity,), jnp.int32).at[position].set(labels)
    out_labels = out_labels.reshape(shard_count, capacity)
    incoming, in_labels = (
        lax.all_to_all(outgoing, "ctx", split_axis=0, concat_axis=0, tiled=True),
        lax.all_to_all(out_labels, "ctx", split_axis=0, concat_axis=0, tiled=True),
    )
    packed = incoming.reshape(-1, incoming.shape[-1])
    owners = in_labels.reshape(-1)
    embedded = jnp.dot(packed, w_embed, preferred_element_type=jnp.float32)
    normed = (
        embedded * lax.rsqrt(jnp.mean(embedded * embedded, axis=-1, keepdims=True) + 1e-06) * gain
    ).astype(jnp.bfloat16)
    heads_here = w_qkv.shape[2] // HEAD
    projected = jnp.dot(
        normed, w_qkv.reshape(w_qkv.shape[0], -1), preferred_element_type=jnp.float32
    )
    projected = projected.reshape(-1, 3, heads_here, HEAD)
    queries = head_norm(projected[:, 0]).astype(jnp.bfloat16)
    keys_own = head_norm(projected[:, 1]).astype(jnp.bfloat16)
    values_own = projected[:, 2].astype(jnp.bfloat16)
    factor = 1.0 / HEAD**0.5
    key_piece = lax.all_gather(keys_own, "ctx", axis=0, tiled=True)
    value_piece = lax.all_gather(values_own, "ctx", axis=0, tiled=True)
    label_piece = lax.all_gather(owners, "ctx", axis=0, tiled=True)
    scores = (
        jnp.einsum("qhd,khd->hqk", queries, key_piece, preferred_element_type=jnp.float32) * factor
    )
    allowed = (owners[:, None] == label_piece[None, :]) & (owners[:, None] > 0)
    expo = jnp.where(allowed[None], jnp.exp(scores), 0.0)
    total = jnp.sum(expo, axis=-1).T
    summed = jnp.einsum(
        "hqk,khd->qhd", expo.astype(jnp.bfloat16), value_piece, preferred_element_type=jnp.float32
    )
    summed, total = (summed, total)
    empty_slot = (owners == 0).astype(jnp.float32)
    attended = summed / (total + empty_slot[:, None])[:, :, None]
    return attended.reshape(1, queries.shape[0], heads_here * HEAD).astype(jnp.bfloat16)


def solution(mesh):
    in_specs = (
        P("section", "ctx", None, None),
        P(),
        P(),
        P(None, "ctx", None),
        P(None, "ctx"),
        P(),
        P(),
        P(None, None, "mp"),
    )
    out_specs = P("section", "ctx", "mp")
    return jax.shard_map(
        on_device, mesh=mesh, in_specs=in_specs, out_specs=out_specs, check_vma=False
    )
```

profile of v0, /device:TPU:1, one launch (start us, length us, event | category | flops | bytes accessed | tf_op | source)
XLA Modules:
  0.0 181.9 jit_solution(528463704101767966)
XLA Ops:
  6.5 1.2 slice_bitcast_fusion.2
  7.7 1.0 slice_bitcast_fusion.3
  8.7 0.8 concatenate.8
  9.6 1.6 fusion.31
  11.2 0.4 convolution_add_fusion.1
  11.7 1.8 convolution_convert_fusion
  14.0 0.2 reduce_window_sum.11
  14.3 0.7 collective-permute-done
  15.0 0.9 scatter_custom_fusion
  15.9 0.7 reshape.205
  16.6 5.7 %all-to-all-start = ((bf16[4,2,1536]{2,1,0:T(2,128)(2,1)}), bf16[4,2,1536]{2,1,0:T(2,128)(2,1)S(1)}, u32[]{:S(2)}, u32[]{:S(2)}) async-start(bf16[4,2,1536]{2,1,0:T(2,128)(2,1)} %reshape.205), calls=%async_computation | async-start | bytes 49152 | tf_op jit(solution)/shard_map/all_to_all | solution.py:73
  22.4 48.7 %copy.10 = bf16[6144,3,1024]{0,2,1:T(8,128)(2,1)} copy(bf16[6144,3,1024]{2,0,1:T(8,128)(2,1)} %param.15) | data formatting | bytes 75497472 | tf_op args[7]
  71.2 2.9 %multiply_reduce_fusion = (f32[192]{0:T(256)S(1)}, f32[192,6144]{1,0:T(8,128)}) fusion(bf16[192,64]{1,0:T(8,128)(2,1)S(1)} %bitcast.92, bf16[64,6144]{1,0:T(8,128)(2,1)S(1)} %copy-done), kind=kOutput, calls=%fused_computation.4 | convolution fusion | flops 153354048 | bytes 5530368 | tf_op jit(solution)/shard_map/dot_general | solution.py:78
  74.1 18.8 %fusion.5 = f32[192,3,8,128]{3,0,2,1:T(8,128)S(1)} fusion(bf16[3,8,128,6144]{3,2,1,0:T(8,128)(2,1)} %bitcast.88, f32[192,6144]{1,0:T(8,128)} %get-tuple-element.10, f32[6144]{0:T(1024)S(1)} %copy-done.5, f32[192]{0:T(256)S(1)} %add_rsqrt_fusion.2), kind=kOutput, calls=%fused_computation.9 | convolution fusion | flops 7251296256 | bytes 44851968 | tf_op jit(solution)/shard_map/dot_general | solution.py:83
  92.9 0.6 multiply_reduce_fusion.2
  93.6 1.0 multiply_convert_fusion.2
  94.7 0.8 slice.71
  95.5 1.0 scatter_custom_fusion.1
  96.5 0.7 all_to_all.10
  97.2 4.5 %all-to-all-start.1 = ((s32[4,1,48]{2,1,0:T(1,128)}), s32[4,1,48]{2,1,0:T(1,128)S(1)}, u32[]{:S(2)}, u32[]{:S(2)}) async-start(s32[4,1,48]{2,1,0:T(1,128)} %all_to_all.10), calls=%async_computation.1 | async-start | bytes 4096 | tf_op jit(solution)/shard_map/all_to_all | solution.py:74
  101.7 0.6 dynamic-slice.1
  102.9 3.2 %all-to-all-done.1 = s32[4,1,48]{2,1,0:T(1,128)S(1)} async-done(((s32[4,1,48]{2,1,0:T(1,128)}), s32[4,1,48]{2,1,0:T(1,128)S(1)}, u32[]{:S(2)}, u32[]{:S(2)}) %all-to-all-start.1) | async-done | bytes 800 | tf_op jit(solution)/shard_map/all_to_all | solution.py:74
  106.1 0.6 broadcast.155
  106.7 0.6 reduce.3
  107.4 0.2 dynamic-update-slice
  107.6 6.2 %all-reduce.2 = s32[768]{0:T(1024)S(1)} all-reduce(s32[768]{0:T(1024)S(1)} %dynamic-update-slice), channel_id=1, replica_groups=mesh['section'=2,'ctx'=4,'mp'=4] {'ctx'}, use_global_device_ids=true, to_apply=%add.2 | all-reduce | flops 768 | bytes 6144
  114.0 18.9 %all-gather.4.cloned.1.call-done = bf16[768,8,128]{2,0,1:T(8,128)(2,1)} async-done(((bf16[192,8,128]{2,0,1:T(8,128)(2,1)}), bf16[768,8,128]{2,0,1:T(8,128)(2,1)}) %all-gather.4.cloned.1.call-update) | async-done | bytes 1572880 | tf_op jit(solution)/shard_map/all_gather | solution.py:91
  132.9 4.8 %fusion = (f32[8,192]{1,0:T(8,128)S(1)}, f32[8,192,768]{2,1,0:T(8,128)}) fusion(pred[192,768]{1,0:T(8,128)(4,1)S(1)} %compare_and_fusion, bf16[768,8,128]{2,0,1:T(8,128)(2,1)} %all-gather.4.cloned.1.call-done, f32[192,3,8,128]{3,0,2,1:T(8,128)S(1)} %fusion.5, f32[192,8]{0,1:T(8,128)S(1)} %add_rsqrt_fusion.1), kind=kOutput, calls=%fused_computation.5 | convolution fusion | flops 305920512 | bytes 7239680 | tf_op jit(solution)/shard_map/qhd,khd->hqk/dot_general | solution.py:95
  137.8 32.2 %all-gather.6.cloned.1.call-done = bf16[768,1,8,128]{3,0,2,1:T(8,128)(2,1)} async-done(((bf16[192,1,8,128]{3,0,2,1:T(8,128)(2,1)}), bf16[768,1,8,128]{3,0,2,1:T(8,128)(2,1)}) %all-gather.6.cloned.1.call-update) | async-done | bytes 1572880 | tf_op jit(solution)/shard_map/all_gather | solution.py:92
  170.0 3.8 %fusion.23 = bf16[192,8,128]{2,0,1:T(8,128)(2,1)S(1)} fusion(bf16[768,1,8,128]{3,0,2,1:T(8,128)(2,1)} %all-gather.6.cloned.1.call-done, f32[8,192,768]{2,1,0:T(8,128)} %get-tuple-element.12, pred[192,768]{1,0:T(8,128)(4,1)S(1)} %compare_and_fusion, f32[192,8]{0,1:T(8,128)S(1)} %add_bitcast_fusion), kind=kOutput, calls=%fused_computation.22 | convolution fusion | flops 305922048 | bytes 6838272 | tf_op jit(solution)/shard_map/hqk,khd->qhd/dot_general | solution.py:100
  173.8 0.3 copy.11
  174.1 0.9 convert_element_type.66
  (39 shorter events, 1.2 us)
Async XLA Ops:
  6.5 64.7 %copy-start = (bf16[64,6144]{1,0:T(8,128)(2,1)S(1)}, bf16[64,6144]{1,0:T(8,128)(2,1)}, u32[]{:S(2)}) copy-start(bf16[64,6144]{1,0:T(8,128)(2,1)} %param.13) | copy-start | bytes 2359300
  6.5 4.7 %copy-start.2 = (bf16[3,512,512]{2,1,0:T(8,128)(2,1)S(1)}, bf16[3,512,512]{2,1,0:T(8,128)(2,1)}, u32[]{:S(2)}) copy-start(bf16[3,512,512]{2,1,0:T(8,128)(2,1)} %param.9) | copy-start | bytes 4718596
  6.5 5.1 %copy-start.6 = (bf16[512,16]{0,1:T(8,128)(2,1)S(1)}, bf16[512,16]{0,1:T(8,128)(2,1)}, u32[]{:S(2)}) copy-start(bf16[512,16]{0,1:T(8,128)(2,1)} %param.10) | copy-start | bytes 49156
  11.2 2.6 %copy-start.3 = (s32[2,128,1]{1,2,0:T(1,128)S(1)}, s32[2,128,1]{1,2,0:T(1,128)}, u32[]{:S(2)}) copy-start(s32[2,128,1]{1,2,0:T(1,128)} %param.11) | copy-start | bytes 3076
  13.7 1.3 collective-permute-start
  16.6 54.5 %all-to-all-start = ((bf16[4,2,1536]{2,1,0:T(2,128)(2,1)}), bf16[4,2,1536]{2,1,0:T(2,128)(2,1)S(1)}, u32[]{:S(2)}, u32[]{:S(2)}) async-start(bf16[4,2,1536]{2,1,0:T(2,128)(2,1)} %reshape.205), calls=%async_computation | async-start | bytes 49152 | tf_op jit(solution)/shard_map/all_to_all | solution.py:73
  22.4 110.6 %all-gather.4.cloned.1.call-start = ((), (), s32[]{:S(2)}) async-start(), calls=%async_computation.2 | async-start | bytes 1966080 | tf_op jit(solution)/shard_map/all_gather | solution.py:91
  71.1 3.0 %copy-start.5 = (f32[6144]{0:T(1024)S(1)}, f32[6144]{0:T(1024)}, u32[]{:S(2)}) copy-start(f32[6144]{0:T(1024)} %param.14) | copy-start | bytes 73732
  74.1 21.4 %copy-start.4 = (s32[2,128]{1,0:T(2,128)S(1)}, s32[2,128]{1,0:T(2,128)}, u32[]{:S(2)}) copy-start(s32[2,128]{1,0:T(2,128)} %param.12) | copy-start | bytes 3076
  74.1 27.6 %copy-start.7 = (u32[32]{0:T(128)S(1)}, u32[32]{0:T(128)}, u32[]{:S(2)}) copy-start(u32[32]{0:T(128)} %constant.76) | copy-start | bytes 388
  94.6 75.4 %all-gather.6.cloned.1.call-start = ((), (), s32[]{:S(2)}) async-start(), calls=%async_computation.3 | async-start | bytes 1966080 | tf_op jit(solution)/shard_map/all_gather | solution.py:92
  97.2 9.0 %all-to-all-start.1 = ((s32[4,1,48]{2,1,0:T(1,128)}), s32[4,1,48]{2,1,0:T(1,128)S(1)}, u32[]{:S(2)}, u32[]{:S(2)}) async-start(s32[4,1,48]{2,1,0:T(1,128)} %all_to_all.10), calls=%async_computation.1 | async-start | bytes 4096 | tf_op jit(solution)/shard_map/all_to_all | solution.py:74
  170.0 5.0 %copy-start.1 = (bf16[64,6144]{1,0:T(8,128)(2,1)S(1)}, bf16[64,6144]{1,0:T(8,128)(2,1)}, u32[]{:S(2)}) copy-start(bf16[64,6144]{1,0:T(8,128)(2,1)} %param.13) | copy-start | bytes 2359300
Sparse Core Ops, SparseCore 0:
  94.7 38.1 all-gather.3
  134.5 35.4 all-gather.5
where the time goes:
time: 185 us; the launch traced here: 182 us
  local copies, waits for them, and re-layouts  58.8 us (32%)
  waiting for transfers between devices  55.1 us (30%)
  matrix products  34.2 us (18%)
  between operations  14.2 us (8%)
  starting transfers between devices  10.4 us (6%)
  blocking collectives  6.19 us (3%)
  other arithmetic  2.92 us (2%)
    unnamed x22, local copies, waits for them, and re-layouts  50.4 us
    all_gather x1, waiting for transfers between devices, on_device(): value_piece = lax.all_gather(values_own, 'ctx', axis=0, tiled=True)  32.2 us
    all_gather x1, waiting for transfers between devices, on_device(): key_piece = lax.all_gather(keys_own, 'ctx', axis=0, tiled=True)  18.9 us
    dot_general x1, matrix products, on_device(): jnp.dot(normed, w_qkv.reshape(w_qkv.shape[0], -1), preferred_element_type...  18.8 us
    unnamed x1, blocking collectives  6.19 us
    all_to_all x1, starting transfers between devices, on_device(): lax.all_to_all(outgoing, 'ctx', split_axis=0, concat_axis=0, tiled=True)  5.74 us
    dot_general x1, matrix products, on_device(): jnp.einsum('qhd,khd->hqk', queries, key_piece, preferred_element_type=jnp...  4.84 us
    all_to_all x1, starting transfers between devices, on_device(): lax.all_to_all(out_labels, 'ctx', split_axis=0, concat_axis=0, tiled=True)  4.53 us
  transfers between devices with their start and end apart: 5, of which 4 were waited for; matrix products, arithmetic and copies ran while one was open for 32% of the time, Pallas kernels for 0%

commit v1 on v0

v1 whole, which is shorter than its diff:
```python
import functools

import jax
import jax.numpy as jnp
from jax import lax
from jax.experimental import pallas as pl
from jax.experimental.pallas import tpu as pltpu
from jax.sharding import PartitionSpec as P

HEAD = 128
GROUP = 4
LANES = 128
META = 16
EPS = 1e-06
MESH = pl.DeviceIdType.MESH
F32 = jnp.float32
BF16 = jnp.bfloat16
ANY = pl.BlockSpec(memory_space=pl.ANY)
VMEM = pl.BlockSpec(memory_space=pltpu.VMEM)


def dot(a, b):
    return jnp.dot(a, b, preferred_element_type=F32)


def dot_nt(a, b):
    return lax.dot_general(a, b, (((1,), (1,)), ((), ())), preferred_element_type=F32)


def iota(shape, dim):
    return lax.broadcasted_iota(jnp.int32, shape, dim)


def encode_kernel(
    shards, frame_count, pieces,
    frames_hbm, conv_hbm, lat_ref, dest_ref, pick_ref, embed_hbm, gain_ref, qkv_hbm,
    rows_out, weff_out,
    frames, conv, embed, qkv, scaled, hidden, outgoing, mine,
    in_sem, qkv_sem, row_send, row_recv, half_send, half_recv, keep_sem,
):
    section = lax.axis_index("section")
    ctx = lax.axis_index("ctx")
    other = 1 - section
    depth = embed.shape[1]
    latent = embed.shape[0]
    half = qkv.shape[2]
    step = depth // pieces
    row_count = outgoing.shape[0] - META

    loads = [
        pltpu.make_async_copy(frames_hbm, frames, in_sem.at[0]),
        pltpu.make_async_copy(conv_hbm, conv, in_sem.at[1]),
        pltpu.make_async_copy(embed_hbm, embed, in_sem.at[2]),
    ]
    for load in loads:
        load.start()
    columns = pl.ds(pl.multiple_of(section * half, LANES), half)
    streams = []
    for j in range(3):
        for p in range(pieces):
            part = pl.ds(p * step, step)
            stream = pltpu.make_async_copy(
                qkv_hbm.at[j, part, columns], qkv.at[j, part, :], qkv_sem.at[j * pieces + p]
            )
            stream.start()
            streams.append(stream)

    barrier = pltpu.get_barrier_semaphore()
    for d in range(shards):
        pl.semaphore_signal(
            barrier, inc=1,
            device_id={"section": other, "ctx": lax.rem(ctx + d, shards)}, device_id_type=MESH,
        )

    first = section == 0
    dest = jnp.where(first, dest_ref[0], dest_ref[1])
    pick = jnp.where(first, pick_ref[0:1, :], pick_ref[1:2, :])
    tier = (pick >= 4).astype(jnp.int32) + (pick >= 6).astype(jnp.int32)
    label = dest // GROUP + shards // GROUP * tier + 1
    padded = -(-shards // 8) * 8
    onehot = (iota((padded, row_count), 0) == dest).astype(F32)
    earlier = (iota((row_count, row_count), 0) < iota((row_count, row_count), 1)).astype(F32)
    before = dot(onehot.astype(BF16), earlier.astype(BF16))
    within = jnp.sum(before * onehot, axis=0, keepdims=True)
    line = iota((META, row_count), 0)
    meta = jnp.where(line == 0, dest.astype(F32), 0.0)
    meta = jnp.where(line == 1, within, meta)
    meta = jnp.where(line == 2, label.astype(F32), meta)
    outgoing[row_count:, :] = meta.astype(BF16)

    loads[0].wait()
    loads[1].wait()
    cells = frames.shape[0]
    frame = cells // frame_count
    hidden[...] = dot(frames[...], conv[0])
    hidden[frame:, :] += dot(frames[: cells - frame, :], conv[1])
    hidden[2 * frame :, :] += dot(frames[: cells - 2 * frame, :], conv[2])
    value = hidden[...]
    active = (value * jax.nn.sigmoid(value)).astype(BF16)
    channels = lat_ref.shape[0]
    per = latent // channels
    narrow = dot_nt(active, lat_ref[...]).astype(BF16)
    lane = iota((channels, LANES), 1)
    spread = ((lane % channels == iota((channels, LANES), 0)) & (lane < latent)).astype(F32)
    wide = dot(narrow, spread.astype(BF16))
    wide = jnp.where(
        iota((cells, LANES), 1) // channels == iota((cells, LANES), 0) % per, wide, 0.0
    ).astype(BF16)
    gather = (iota((row_count, cells), 1) // per == iota((row_count, cells), 0)).astype(F32)
    patches = dot(gather.astype(BF16), wide)
    loads[2].wait()
    narrow_patches = patches[:, :latent].astype(BF16)
    square = jnp.zeros((row_count, LANES), F32)
    tile = 512
    for k in range(depth // tile):
        x = dot(narrow_patches, embed[:, k * tile : (k + 1) * tile])
        x = x * x
        for i in range(tile // LANES):
            square = square + x[:, i * LANES : (i + 1) * LANES]
    scale = lax.rsqrt(jnp.sum(square, axis=1, keepdims=True) / depth + EPS)
    high = scale.astype(BF16).astype(F32)
    middle = (scale - high).astype(BF16).astype(F32)
    low = scale - high - middle
    lane = iota((row_count, LANES), 1)
    message = jnp.where(lane == latent, high, patches)
    message = jnp.where(lane == latent + 1, middle, message)
    message = jnp.where(lane == latent + 2, low, message)
    outgoing[:row_count, :] = message.astype(BF16)

    pl.semaphore_wait(barrier, shards)
    sends = []
    for d in range(shards):
        send = pltpu.make_async_remote_copy(
            src_ref=outgoing, dst_ref=rows_out.at[ctx],
            send_sem=row_send.at[d], recv_sem=row_recv.at[d],
            device_id={"section": other, "ctx": lax.rem(ctx + d, shards)}, device_id_type=MESH,
        )
        send.start()
        sends.append(send)

    for k in range(depth // tile):
        part = slice(k * tile, (k + 1) * tile)
        full = embed[:, part].astype(F32) * gain_ref[:, part]
        top = full.astype(BF16)
        scaled[:latent, part] = top
        scaled[latent:, part] = (full - top.astype(F32)).astype(BF16)

    keeps = []
    for j in range(3):
        total = jnp.zeros((2 * latent, half), F32)
        for p in range(pieces):
            streams[j * pieces + p].wait()
            part = slice(p * step, (p + 1) * step)
            total = total + dot(scaled[:, part], qkv[j, part, :])
        mine[j] = (total[:latent] + total[latent:]).astype(BF16)
        send = pltpu.make_async_remote_copy(
            src_ref=mine.at[j], dst_ref=weff_out.at[section, j],
            send_sem=half_send.at[j], recv_sem=half_recv.at[j],
            device_id={"section": other}, device_id_type=MESH,
        )
        send.start()
        sends.append(send)
        keep = pltpu.make_async_copy(mine.at[j], weff_out.at[section, j], keep_sem.at[j])
        keep.start()
        keeps.append(keep)
    for keep in keeps:
        keep.wait()
    for send in sends:
        send.wait()


def attend_kernel(shards, capacity, rows_ref, weff_ref, out_ref, picked_ref, row_ref, mask_ref):
    ctx = lax.axis_index("ctx")
    row_count = rows_ref.shape[1] - META
    latent = weff_ref.shape[2]
    half = weff_ref.shape[3]
    slots = out_ref.shape[0]
    total_rows = shards * row_count

    @pl.when(pl.program_id(0) == 0)
    def _():
        labels, spots = [], []
        for source in range(shards):
            meta = rows_ref[source, row_count:, :].astype(F32)
            labels.append(meta[2:3, :])
            home = meta[1:2, :] + (source * capacity)
            spots.append(jnp.where(meta[0:1, :] == ctx.astype(F32), home, -1.0))
            row_ref[source * row_count : (source + 1) * row_count, :] = rows_ref[source, :row_count, :]
        label = jnp.concatenate(labels, axis=1)
        spot = jnp.concatenate(spots, axis=1).astype(jnp.int32)
        taken = spot == iota((slots, total_rows), 0)
        picked_ref[...] = dot(taken.astype(F32).astype(BF16), row_ref[...]).astype(BF16)
        own = jnp.sum(jnp.where(taken, label, 0.0), axis=1, keepdims=True)
        mask_ref[...] = (label == own).astype(F32)

    def scale_of(block):
        return (
            block[:, latent : latent + 1].astype(F32)
            + block[:, latent + 1 : latent + 2].astype(F32)
            + block[:, latent + 2 : latent + 3].astype(F32)
        )

    def head_norm(x):
        return x * lax.rsqrt(jnp.mean(x * x, axis=-1, keepdims=True) + EPS)

    picked = picked_ref[...]
    everything = row_ref[...]
    picked_scale = scale_of(picked)
    row_scale = scale_of(everything)
    q = dot(picked[:, :latent], weff_ref[0, 0])
    k = dot(everything[:, :latent], weff_ref[0, 1])
    v = dot(everything[:, :latent], weff_ref[0, 2])
    allowed = mask_ref[...] > 0.5
    factor = 1.0 / HEAD**0.5
    for h in range(half // HEAD):
        part = slice(h * HEAD, (h + 1) * HEAD)
        queries = head_norm(q[:, part] * picked_scale).astype(BF16)
        keys = head_norm(k[:, part] * row_scale).astype(BF16)
        values = (v[:, part] * row_scale).astype(BF16)
        scores = dot_nt(queries, keys) * factor
        expo = jnp.where(allowed, jnp.exp(scores), 0.0)
        den = jnp.sum(expo, axis=1, keepdims=True)
        summed = dot(expo.astype(BF16), values)
        out_ref[:, part] = (summed / jnp.where(den > 0.0, den, 1.0)).astype(BF16)


def on_device(shards, sections, frames, w_conv, w_lat, dest, pick, w_embed, gain, w_qkv):
    _, frame_count, frame, channels = frames.shape
    latent, depth = w_embed.shape
    cells = frame_count * frame
    row_count = dest.shape[1]
    columns = w_qkv.shape[2]
    half = columns // sections
    pieces = 4
    capacity = max(2, 3 * row_count // (2 * shards))
    slots = shards * capacity
    rows, weff = pl.pallas_call(
        functools.partial(encode_kernel, shards, frame_count, pieces),
        out_shape=(
            jax.ShapeDtypeStruct((shards, row_count + META, LANES), BF16),
            jax.ShapeDtypeStruct((sections, 3, latent, half), BF16),
        ),
        in_specs=[ANY, ANY, VMEM, VMEM, VMEM, ANY, VMEM, ANY],
        out_specs=(ANY, ANY),
        scratch_shapes=[
            pltpu.VMEM((cells, channels), BF16),
            pltpu.VMEM(w_conv.shape, BF16),
            pltpu.VMEM((latent, depth), BF16),
            pltpu.VMEM((3, depth, half), BF16),
            pltpu.VMEM((2 * latent, depth), BF16),
            pltpu.VMEM((cells, channels), F32),
            pltpu.VMEM((row_count + META, LANES), BF16),
            pltpu.VMEM((3, latent, half), BF16),
            pltpu.SemaphoreType.DMA((3,)),
            pltpu.SemaphoreType.DMA((3 * pieces,)),
            pltpu.SemaphoreType.DMA((shards,)),
            pltpu.SemaphoreType.DMA((shards,)),
            pltpu.SemaphoreType.DMA((3,)),
            pltpu.SemaphoreType.DMA((3,)),
            pltpu.SemaphoreType.DMA((3,)),
        ],
        compiler_params=pltpu.CompilerParams(
            collective_id=0, has_side_effects=True, vmem_limit_bytes=48 << 20
        ),
    )(
        frames.reshape(cells, channels),
        w_conv,
        w_lat.T,
        dest.transpose(0, 2, 1),
        pick,
        w_embed,
        gain.reshape(1, depth),
        w_qkv.transpose(1, 0, 2),
    )
    out = pl.pallas_call(
        functools.partial(attend_kernel, shards, capacity),
        grid=(sections,),
        out_shape=jax.ShapeDtypeStruct((slots, columns), BF16),
        in_specs=[
            pl.BlockSpec((shards, row_count + META, LANES), lambda i: (0, 0, 0)),
            pl.BlockSpec((1, 3, latent, half), lambda i: (i, 0, 0, 0)),
        ],
        out_specs=pl.BlockSpec((slots, half), lambda i: (0, i)),
        scratch_shapes=[
            pltpu.VMEM((slots, LANES), BF16),
            pltpu.VMEM((shards * row_count, LANES), BF16),
            pltpu.VMEM((slots, shards * row_count), F32),
        ],
        compiler_params=pltpu.CompilerParams(vmem_limit_bytes=48 << 20),
    )(rows, weff)
    return out.reshape(1, slots, columns)


def solution(mesh):
    in_specs = (
        P("section", "ctx", None, None),
        P(),
        P(),
        P(None, "ctx", None),
        P(None, "ctx"),
        P(),
        P(),
        P(None, None, "mp"),
    )
    return jax.shard_map(
        functools.partial(on_device, mesh.shape["ctx"], mesh.shape["section"]),
        mesh=mesh,
        in_specs=in_specs,
        out_specs=P("section", "ctx", "mp"),
        check_vma=False,
    )
```

time: 185 us -> 21.7 us (0.12)
  the two profiles are of different devices: /device:TPU:1 before, /device:TPU:0 now
where the time goes in v1:
time: 21.7 us; the launch traced here: 21.4 us
  Pallas kernels  14.9 us (69%)
  local copies, waits for them, and re-layouts  6.39 us (29%)
    pallas_call x1, Pallas kernels, on_device(): pl.pallas_call(functools.partial(encode_kernel, shards, frame_count, piec...  10.6 us
    unnamed x14, local copies, waits for them, and re-layouts  6.39 us
    pallas_call x1, Pallas kernels, on_device(): pl.pallas_call(functools.partial(attend_kernel, shards, capacity), grid=(...  4.33 us

profile of v1, /device:TPU:0, one launch (start us, length us, event | category | flops | bytes accessed | tf_op | source)
XLA Modules:
  0.0 21.4 jit_solution(11370155249835230904)
XLA Ops:
  0.0 0.0 copy-start
  0.0 1.4 %copy-done = bf16[3,512,512]{2,1,0:T(8,128)(2,1)S(1)} copy-done((bf16[3,512,512]{2,1,0:T(8,128)(2,1)S(1)}, bf16[3,512,512]{2,1,0:T(8,128)(2,1)}, u32[]{:S(2)}) %copy-start) | copy-done | bytes 1572888
  1.4 0.0 copy-start.1
  1.4 1.1 %copy-done.1 = bf16[64,6144]{1,0:T(8,128)(2,1)S(1)} copy-done((bf16[64,6144]{1,0:T(8,128)(2,1)S(1)}, bf16[64,6144]{1,0:T(8,128)(2,1)}, u32[]{:S(2)}) %copy-start.1) | copy-done | bytes 786456
  2.5 0.0 copy-start.2
  2.5 1.0 %copy-done.2 = bf16[1,4,128,512]{3,2,1,0:T(8,128)(2,1)S(1)} copy-done((bf16[1,4,128,512]{3,2,1,0:T(8,128)(2,1)S(1)}, bf16[1,4,128,512]{3,2,1,0:T(8,128)(2,1)}, u32[]{:S(2)}) %copy-start.2) | copy-done | bytes 524312
  3.6 0.0 copy-start.3
  3.6 0.7 %copy-done.3 = f32[6144]{0:T(1024)S(1)} copy-done((f32[6144]{0:T(1024)S(1)}, f32[6144]{0:T(1024)}, u32[]{:S(2)}) %copy-start.3) | copy-done | bytes 24600
  4.3 0.0 copy-start.4
  4.3 0.7 %copy-done.4 = bf16[512,16]{0,1:T(8,128)(2,1)S(1)} copy-done((bf16[512,16]{0,1:T(8,128)(2,1)S(1)}, bf16[512,16]{0,1:T(8,128)(2,1)}, u32[]{:S(2)}) %copy-start.4) | copy-done | bytes 16408
  5.0 0.0 copy-start.5
  5.0 0.7 %copy-done.5 = s32[2,128,1]{1,2,0:T(1,128)S(1)} copy-done((s32[2,128,1]{1,2,0:T(1,128)S(1)}, s32[2,128,1]{1,2,0:T(1,128)}, u32[]{:S(2)}) %copy-start.5) | copy-done | bytes 1048
  5.7 0.0 copy-start.6
  5.7 0.7 %copy-done.6 = s32[2,128]{1,0:T(2,128)S(1)} copy-done((s32[2,128]{1,0:T(2,128)S(1)}, s32[2,128]{1,0:T(2,128)}, u32[]{:S(2)}) %copy-start.6) | copy-done | bytes 1048
  6.4 10.6 %shard_map.82 = (bf16[4,144,128]{2,1,0:T(8,128)(2,1)S(1)}, bf16[2,3,64,512]{3,2,1,0:T(8,128)(2,1)S(1)}) custom-call(bf16[512,512]{1,0:T(8,128)(2,1)S(1)} %bitcast.6, bf16[3,512,512]{2,1,0:T(8,128)(2,1)S(1)} %copy-done, bf16[16,512]{1,0:T(8,128)(2,1)S(1)} %bitcast.8, s32[2,1,128]{2,1,0:T(1,128)S(1)} %bitcast.9, s32[2,128]{1,0:T(2,128)S(1)} %copy-done.6, ...), custom_call_target="tpu_custom_call" | custom-call | tf_op jit(solution)/shard_map/pallas_call | solution.py:237
  17.0 4.3 %shard_map.83 = bf16[192,1024]{1,0:T(8,128)(2,1)} custom-call(bf16[4,144,128]{2,1,0:T(8,128)(2,1)S(1)} %get-tuple-element.7.rows_ref, bf16[2,3,64,512]{3,2,1,0:T(8,128)(2,1)S(1)} %get-tuple-element.8.weff_ref), custom_call_target="tpu_custom_call" | custom-call | tf_op jit(solution)/shard_map/pallas_call | solution.py:275
Async XLA Ops:
  0.0 1.4 %copy-start = (bf16[3,512,512]{2,1,0:T(8,128)(2,1)S(1)}, bf16[3,512,512]{2,1,0:T(8,128)(2,1)}, u32[]{:S(2)}) copy-start(bf16[3,512,512]{2,1,0:T(8,128)(2,1)} %conv_hbm.1) | copy-start | bytes 4718596
  1.4 1.1 %copy-start.1 = (bf16[64,6144]{1,0:T(8,128)(2,1)S(1)}, bf16[64,6144]{1,0:T(8,128)(2,1)}, u32[]{:S(2)}) copy-start(bf16[64,6144]{1,0:T(8,128)(2,1)} %embed_hbm.1) | copy-start | bytes 2359300
  2.5 1.0 %copy-start.2 = (bf16[1,4,128,512]{3,2,1,0:T(8,128)(2,1)S(1)}, bf16[1,4,128,512]{3,2,1,0:T(8,128)(2,1)}, u32[]{:S(2)}) copy-start(bf16[1,4,128,512]{3,2,1,0:T(8,128)(2,1)} %param.8) | copy-start | bytes 1572868
  3.6 0.7 %copy-start.3 = (f32[6144]{0:T(1024)S(1)}, f32[6144]{0:T(1024)}, u32[]{:S(2)}) copy-start(f32[6144]{0:T(1024)} %param.14) | copy-start | bytes 73732
  4.3 0.7 %copy-start.4 = (bf16[512,16]{0,1:T(8,128)(2,1)S(1)}, bf16[512,16]{0,1:T(8,128)(2,1)}, u32[]{:S(2)}) copy-start(bf16[512,16]{0,1:T(8,128)(2,1)} %param.10) | copy-start | bytes 49156
  5.0 0.7 %copy-start.5 = (s32[2,128,1]{1,2,0:T(1,128)S(1)}, s32[2,128,1]{1,2,0:T(1,128)}, u32[]{:S(2)}) copy-start(s32[2,128,1]{1,2,0:T(1,128)} %param.11) | copy-start | bytes 3076
  5.7 0.7 %copy-start.6 = (s32[2,128]{1,0:T(2,128)S(1)}, s32[2,128]{1,0:T(2,128)}, u32[]{:S(2)}) copy-start(s32[2,128]{1,0:T(2,128)} %pick_ref.1) | copy-start | bytes 3076

commit v2 on v1

v2 whole, which is shorter than its diff:
```python
import functools
import math

import jax
import jax.numpy as jnp
from jax import lax
from jax.experimental import pallas as pl
from jax.experimental.pallas import tpu as pltpu
from jax.sharding import PartitionSpec as P

HEAD = 128
GROUP = 4
LANES = 128
META = 16
EPS = 1e-06
BARRED = 16384.0
LOG2E = math.log2(math.e)
SPLIT = True
MESH = pl.DeviceIdType.MESH
F32 = jnp.float32
BF16 = jnp.bfloat16
HBM = pl.BlockSpec(memory_space=pltpu.HBM)


def dot(a, b):
    return jnp.dot(a, b, preferred_element_type=F32)


def dot_nt(a, b):
    return lax.dot_general(a, b, (((1,), (1,)), ((), ())), preferred_element_type=F32)


def iota(shape, dim):
    return lax.broadcasted_iota(jnp.int32, shape, dim)


def layer_kernel(
    shards, frame_count, pieces, capacity, split,
    frames_hbm, conv_hbm, lat_hbm, dest_hbm, pick_hbm, embed_hbm, gain_hbm, qkv_hbm,
    out_hbm,
    frames, conv, lat_ref, dest_ref, pick_ref, embed, gain_ref, qkv, scaled, hidden, outgoing, arrived, mine, theirs,
    scales, floors, tags, keys_ref, values_ref, result,
    in_sem, qkv_sem, row_send, row_recv, half_send, half_recv, out_sem,
):
    section = lax.axis_index("section")
    ctx = lax.axis_index("ctx")
    other = 1 - section
    depth = embed.shape[1]
    latent = embed.shape[0]
    half = qkv.shape[2]
    step = depth // pieces
    row_count = outgoing.shape[0] - META

    loads = [
        pltpu.make_async_copy(source, target, in_sem.at[i])
        for i, (source, target) in enumerate((
            (embed_hbm, embed), (gain_hbm, gain_ref), (dest_hbm, dest_ref), (pick_hbm, pick_ref),
            (frames_hbm, frames), (conv_hbm, conv), (lat_hbm, lat_ref),
        ))
    ]
    for load in loads:
        load.start()
    columns = pl.ds(pl.multiple_of(section * half, LANES), half)
    streams = []
    for j in range(3):
        for p in range(pieces):
            part = pl.ds(p * step, step)
            stream = pltpu.make_async_copy(
                qkv_hbm.at[j, part, columns], qkv.at[j, part, :], qkv_sem.at[j * pieces + p]
            )
            stream.start()
            streams.append(stream)

    barrier = pltpu.get_barrier_semaphore()
    for d in range(shards):
        pl.semaphore_signal(
            barrier, inc=1,
            device_id={"section": other, "ctx": lax.rem(ctx + d, shards)}, device_id_type=MESH,
        )

    loads[0].wait()
    loads[1].wait()
    tile = 512
    for k in range(depth // tile):
        part = slice(k * tile, (k + 1) * tile)
        full = embed[:, part].astype(F32) * gain_ref[:, part]
        top = full.astype(BF16)
        scaled[:latent, part] = top
        if split:
            scaled[latent:, part] = (full - top.astype(F32)).astype(BF16)

    loads[2].wait()
    loads[3].wait()
    first = section == 0
    dest = jnp.where(first, dest_ref[0], dest_ref[1])
    pick = jnp.where(first, pick_ref[0:1, :], pick_ref[1:2, :])
    tier = (pick >= 4).astype(jnp.int32) + (pick >= 6).astype(jnp.int32)
    label = dest // GROUP + shards // GROUP * tier + 1
    padded = -(-shards // 8) * 8
    onehot = (iota((padded, row_count), 0) == dest).astype(F32)
    earlier = (iota((row_count, row_count), 0) < iota((row_count, row_count), 1)).astype(F32)
    before = dot(onehot.astype(BF16), earlier.astype(BF16))
    within = jnp.sum(before * onehot, axis=0, keepdims=True)
    line = iota((META, row_count), 0)
    meta = jnp.where(line == 0, dest.astype(F32), 0.0)
    meta = jnp.where(line == 1, within, meta)
    meta = jnp.where(line == 2, label.astype(F32), meta)
    outgoing[row_count:, :] = meta.astype(BF16)

    loads[4].wait()
    loads[5].wait()
    cells = frames.shape[0]
    frame = cells // frame_count
    hidden[...] = dot(frames[...], conv[0])
    hidden[frame:, :] += dot(frames[: cells - frame, :], conv[1])
    hidden[2 * frame :, :] += dot(frames[: cells - 2 * frame, :], conv[2])
    value = hidden[...]
    active = (value * jax.nn.sigmoid(value)).astype(BF16)
    loads[6].wait()
    channels = lat_ref.shape[0]
    per = latent // channels
    narrow = dot_nt(active, lat_ref[...]).astype(BF16)
    lane = iota((channels, LANES), 1)
    spread = ((lane % channels == iota((channels, LANES), 0)) & (lane < latent)).astype(F32)
    wide = dot(narrow, spread.astype(BF16))
    wide = jnp.where(
        iota((cells, LANES), 1) // channels == iota((cells, LANES), 0) % per, wide, 0.0
    ).astype(BF16)
    gather = (iota((row_count, cells), 1) // per == iota((row_count, cells), 0)).astype(F32)
    patches = dot(gather.astype(BF16), wide)
    narrow_patches = patches[:, :latent].astype(BF16)
    square = jnp.zeros((row_count, LANES), F32)
    for k in range(depth // tile):
        x = dot(narrow_patches, embed[:, k * tile : (k + 1) * tile])
        x = x * x
        for i in range(tile // LANES):
            square = square + x[:, i * LANES : (i + 1) * LANES]
    scale = lax.rsqrt(jnp.sum(square, axis=1, keepdims=True) / depth + EPS)
    high = scale.astype(BF16).astype(F32)
    middle = (scale - high).astype(BF16).astype(F32)
    low = scale - high - middle
    lane = iota((row_count, LANES), 1)
    line = iota((row_count, LANES), 0)
    placed = jnp.where(line == latent + 3, label, 0).astype(F32).astype(BF16)
    message = patches + dot_nt((line == lane).astype(F32).astype(BF16), placed)
    message = jnp.where(lane == latent, high, message)
    message = jnp.where(lane == latent + 1, middle, message)
    message = jnp.where(lane == latent + 2, low, message)
    outgoing[:row_count, :] = message.astype(BF16)

    pl.semaphore_wait(barrier, shards)
    sends = []
    for d in range(shards):
        send = pltpu.make_async_remote_copy(
            src_ref=outgoing, dst_ref=arrived.at[ctx],
            send_sem=row_send.at[d], recv_sem=row_recv.at[d],
            device_id={"section": other, "ctx": lax.rem(ctx + d, shards)}, device_id_type=MESH,
        )
        send.start()
        sends.append(send)

    halves = []
    for j in range(3):
        total = jnp.zeros((scaled.shape[0], half), F32)
        for p in range(pieces):
            streams[j * pieces + p].wait()
            part = slice(p * step, (p + 1) * step)
            total = total + dot(scaled[:, part], qkv[j, part, :])
        if split:
            total = total[:latent] + total[latent:]
        mine[j] = total.astype(BF16)
        send = pltpu.make_async_remote_copy(
            src_ref=mine.at[j], dst_ref=theirs.at[j],
            send_sem=half_send.at[j], recv_sem=half_recv.at[j],
            device_id={"section": other}, device_id_type=MESH,
        )
        send.start()
        halves.append(send)

    for send in sends:
        send.wait()
    slots = shards * capacity
    mine_here = ctx.astype(F32)
    spots = []
    lane = iota((row_count, LANES), 1)

    def constants(block):
        scale = (
            block[:, latent : latent + 1].astype(F32)
            + block[:, latent + 1 : latent + 2].astype(F32)
            + block[:, latent + 2 : latent + 3].astype(F32)
        )
        return scale, block[:, latent + 3 : latent + 4].astype(F32).astype(jnp.int32)

    for source in range(shards):
        meta = arrived[source, row_count:, :].astype(F32)
        spots.append(jnp.where(meta[0:1, :] == mine_here, meta[1:2, :] + source * capacity, -1.0))
        scale, tag = constants(arrived[source, :row_count, :])
        part = slice(source * row_count, (source + 1) * row_count)
        scales[part, :] = jnp.broadcast_to(scale, (row_count, LANES))
        floors[part, :] = jnp.broadcast_to(HEAD * EPS / (scale * scale), (row_count, LANES))
        tags[part, :] = (lane == tag).astype(F32).astype(BF16)
    picked = jnp.zeros((slots, LANES), F32)
    for source in range(shards):
        taken = spots[source].astype(jnp.int32) == iota((slots, row_count), 0)
        picked = picked + dot(taken.astype(F32).astype(BF16), arrived[source, :row_count, :])
    picked = picked.astype(BF16)
    picked_scale, picked_tag = constants(picked)
    picked_scale = jnp.where(picked_tag > 0, picked_scale, 1.0)
    picked_floor = HEAD * EPS / (picked_scale * picked_scale)
    barred = jnp.where(iota((slots, LANES), 1) == picked_tag, 0.0, -BARRED).astype(BF16)
    barred = jnp.where(picked_tag > 0, barred.astype(F32), -BARRED).astype(BF16)
    ones = jnp.ones((shards * row_count, HEAD), BF16)
    gain_q = HEAD**0.5 * LOG2E

    writes = []
    for side, weff in ((0, mine), (1, theirs)):
        if side == 1:
            for send in halves:
                send.wait()
        width = min(half, 2 * HEAD)
        for group in range(half // width):
            part = slice(group * width, (group + 1) * width)
            for source in range(shards):
                block = arrived[source, :row_count, :latent]
                k = dot(block, weff[1, :, part])
                v = dot(block, weff[2, :, part])
                rows = slice(source * row_count, (source + 1) * row_count)
                for h in range(width // HEAD):
                    kh = k[:, h * HEAD : (h + 1) * HEAD]
                    power = jnp.sum(kh * kh, axis=1, keepdims=True) + floors[rows, :]
                    keys_ref[group * (width // HEAD) + h, rows, :] = (kh * lax.rsqrt(power)).astype(BF16)
                    vh = v[:, h * HEAD : (h + 1) * HEAD]
                    values_ref[group * (width // HEAD) + h, rows, :] = (vh * scales[rows, :]).astype(BF16)
            q = dot(picked[:, :latent], weff[0, :, part])
            for h in range(width // HEAD):
                head = group * (width // HEAD) + h
                qh = q[:, h * HEAD : (h + 1) * HEAD]
                power = jnp.sum(qh * qh, axis=1, keepdims=True) + picked_floor
                queries = (qh * (lax.rsqrt(power) * gain_q)).astype(BF16)
                scores = dot_nt(
                    jnp.concatenate([queries, barred], axis=1),
                    jnp.concatenate([keys_ref[head], tags[...]], axis=1),
                )
                weights = jnp.exp2(scores).astype(BF16)
                both = dot(weights, jnp.concatenate([values_ref[head], ones], axis=1))
                den = both[:, HEAD:]
                result[side, :, head * HEAD : (head + 1) * HEAD] = (
                    both[:, :HEAD] / jnp.where(den > 0.0, den, 1.0)
                ).astype(BF16)
        where = pl.ds(pl.multiple_of((section if side == 0 else other) * half, LANES), half)
        write = pltpu.make_async_copy(result.at[side], out_hbm.at[:, where], out_sem.at[side])
        write.start()
        writes.append(write)
    for write in writes:
        write.wait()


def on_device(shards, sections, frames, w_conv, w_lat, dest, pick, w_embed, gain, w_qkv):
    _, frame_count, frame, channels = frames.shape
    latent, depth = w_embed.shape
    cells = frame_count * frame
    row_count = dest.shape[1]
    columns = w_qkv.shape[2]
    half = columns // sections
    pieces = 4
    split = SPLIT
    capacity = max(2, 3 * row_count // (2 * shards))
    slots = shards * capacity
    total_rows = shards * row_count
    out = pl.pallas_call(
        functools.partial(layer_kernel, shards, frame_count, pieces, capacity, split),
        out_shape=jax.ShapeDtypeStruct((slots, columns), BF16),
        in_specs=[HBM] * 8,
        out_specs=HBM,
        scratch_shapes=[
            pltpu.VMEM((cells, channels), BF16),
            pltpu.VMEM(w_conv.shape, BF16),
            pltpu.VMEM((w_lat.shape[1], channels), BF16),
            pltpu.VMEM((sections, 1, row_count), jnp.int32),
            pltpu.VMEM((sections, row_count), jnp.int32),
            pltpu.VMEM((latent, depth), BF16),
            pltpu.VMEM((1, depth), F32),
            pltpu.VMEM((3, depth, half), BF16),
            pltpu.VMEM((2 * latent if split else latent, depth), BF16),
            pltpu.VMEM((cells, channels), F32),
            pltpu.VMEM((row_count + META, LANES), BF16),
            pltpu.VMEM((shards, row_count + META, LANES), BF16),
            pltpu.VMEM((3, latent, half), BF16),
            pltpu.VMEM((3, latent, half), BF16),
            pltpu.VMEM((total_rows, LANES), F32),
            pltpu.VMEM((total_rows, LANES), F32),
            pltpu.VMEM((total_rows, LANES), BF16),
            pltpu.VMEM((half // HEAD, total_rows, HEAD), BF16),
            pltpu.VMEM((half // HEAD, total_rows, HEAD), BF16),
            pltpu.VMEM((sections, slots, half), BF16),
            pltpu.SemaphoreType.DMA((7,)),
            pltpu.SemaphoreType.DMA((3 * pieces,)),
            pltpu.SemaphoreType.DMA((shards,)),
            pltpu.SemaphoreType.DMA((shards,)),
            pltpu.SemaphoreType.DMA((3,)),
            pltpu.SemaphoreType.DMA((3,)),
            pltpu.SemaphoreType.DMA((2,)),
        ],
        compiler_params=pltpu.CompilerParams(
            collective_id=0, has_side_effects=True, vmem_limit_bytes=67043328
        ),
    )(
        frames.reshape(cells, channels),
        w_conv,
        w_lat.T,
        dest.transpose(0, 2, 1),
        pick,
        w_embed,
        gain.reshape(1, depth),
        w_qkv.transpose(1, 0, 2),
    )
    return out.reshape(1, slots, columns)


def solution(mesh):
    in_specs = (
        P("section", "ctx", None, None),
        P(),
        P(),
        P(None, "ctx", None),
        P(None, "ctx"),
        P(),
        P(),
        P(None, None, "mp"),
    )
    return jax.shard_map(
        functools.partial(on_device, mesh.shape["ctx"], mesh.shape["section"]),
        mesh=mesh,
        in_specs=in_specs,
        out_specs=P("section", "ctx", "mp"),
        check_vma=False,
    )
```

time: 21.7 us -> 22.6 us (1.041)
  the two profiles are of different devices: /device:TPU:0 before, /device:TPU:1 now
where the time goes in v2:
time: 22.6 us; the launch traced here: 22.5 us
  Pallas kernels  20.7 us (92%)
  local copies, waits for them, and re-layouts  1.77 us (8%)
    pallas_call x1, Pallas kernels, on_device(): pl.pallas_call(functools.partial(layer_kernel, shards, frame_count, piece...  20.7 us
    unnamed x1, local copies, waits for them, and re-layouts  1.77 us

profile of v2, /device:TPU:1, one launch (start us, length us, event | category | flops | bytes accessed | tf_op | source)
XLA Modules:
  0.0 22.5 jit_solution(4931836191325671659)
XLA Ops:
  0.0 20.7 %shard_map.82 = bf16[192,1024]{1,0:T(8,128)(2,1)} custom-call(bf16[512,512]{1,0:T(8,128)(2,1)} %bitcast.8, bf16[3,512,512]{2,1,0:T(8,128)(2,1)} %conv_hbm.1, bf16[16,512]{1,0:T(8,128)(2,1)} %bitcast.10, s32[2,1,128]{2,1,0:T(1,128)} %bitcast.11, s32[2,128]{1,0:T(2,128)} %pick_hbm.1, bf16[64,6144]{1,0:T(8,128)(2,1)} %embed_hbm.1, f32[1,6144]{1,0:T(1,128)} %bitcast.9, ...), custom_call_target="tpu_custom_call" | custom-call | tf_op jit(solution)/shard_map/pallas_call | solution.py:271
  20.7 1.8 %copy.10 = bf16[1,192,1024]{2,1,0:T(8,128)(2,1)} copy(bf16[1,192,1024]{2,1,0:T(8,128)(2,1)} %bitcast.7) | data formatting | bytes 786432

commit v3 on v1

v3 whole, which is shorter than its diff:
```python
import functools
import math

import jax
import jax.numpy as jnp
from jax import lax
from jax.experimental import pallas as pl
from jax.experimental.pallas import tpu as pltpu
from jax.sharding import PartitionSpec as P

HEAD = 128
GROUP = 4
LANES = 128
META = 16
EPS = 1e-06
BARRED = 16384.0
LOG2E = math.log2(math.e)
SPLIT = True
MESH = pl.DeviceIdType.MESH
F32 = jnp.float32
BF16 = jnp.bfloat16
HBM = pl.BlockSpec(memory_space=pltpu.HBM)


def dot(a, b):
    return jnp.dot(a, b, preferred_element_type=F32)


def dot_nt(a, b):
    return lax.dot_general(a, b, (((1,), (1,)), ((), ())), preferred_element_type=F32)


def iota(shape, dim):
    return lax.broadcasted_iota(jnp.int32, shape, dim)


def encode_kernel(
    shards, frame_count, pieces, split,
    frames_hbm, conv_hbm, lat_hbm, dest_hbm, pick_hbm, embed_hbm, gain_hbm, qkv_hbm,
    rows_out, weff_out,
    frames, conv, lat_ref, dest_ref, pick_ref, embed, gain_ref, qkv, scaled, hidden, outgoing, mine, total,
    in_sem, qkv_sem, row_send, row_recv, half_send, half_recv, keep_sem,
):
    section = lax.axis_index("section")
    ctx = lax.axis_index("ctx")
    other = 1 - section
    depth = embed.shape[1]
    latent = embed.shape[0]
    half = qkv.shape[2]
    step = depth // pieces
    row_count = outgoing.shape[0] - META

    loads = [
        pltpu.make_async_copy(source, target, in_sem.at[i])
        for i, (source, target) in enumerate((
            (embed_hbm, embed), (gain_hbm, gain_ref), (dest_hbm, dest_ref), (pick_hbm, pick_ref),
            (frames_hbm, frames), (conv_hbm, conv), (lat_hbm, lat_ref),
        ))
    ]
    for load in loads:
        load.start()
    columns = pl.ds(pl.multiple_of(section * half, LANES), half)

    def stream(j, p):
        part = pl.ds(pl.multiple_of(p * step, step), step)
        return pltpu.make_async_copy(
            qkv_hbm.at[j, part, columns], qkv.at[j, part, :], qkv_sem.at[j * pieces + p]
        )

    for j in range(3):
        for p in range(pieces):
            stream(j, p).start()

    barrier = pltpu.get_barrier_semaphore()
    for d in range(shards):
        pl.semaphore_signal(
            barrier, inc=1,
            device_id={"section": other, "ctx": lax.rem(ctx + d, shards)}, device_id_type=MESH,
        )

    loads[0].wait()
    loads[1].wait()
    tile = 512

    def scale_part(k, carry):
        part = pl.ds(pl.multiple_of(k * tile, tile), tile)
        full = embed[:, part].astype(F32) * gain_ref[:, part]
        top = full.astype(BF16)
        scaled[:latent, part] = top
        if split:
            scaled[latent:, part] = (full - top.astype(F32)).astype(BF16)
        return carry

    lax.fori_loop(0, depth // tile, scale_part, 0)

    loads[2].wait()
    loads[3].wait()
    first = section == 0
    dest = jnp.where(first, dest_ref[0], dest_ref[1])
    pick = jnp.where(first, pick_ref[0:1, :], pick_ref[1:2, :])
    tier = (pick >= 4).astype(jnp.int32) + (pick >= 6).astype(jnp.int32)
    label = dest // GROUP + shards // GROUP * tier + 1
    padded = -(-shards // 8) * 8
    onehot = (iota((padded, row_count), 0) == dest).astype(F32)
    earlier = (iota((row_count, row_count), 0) < iota((row_count, row_count), 1)).astype(F32)
    before = dot(onehot.astype(BF16), earlier.astype(BF16))
    within = jnp.sum(before * onehot, axis=0, keepdims=True)
    line = iota((META, row_count), 0)
    meta = jnp.where(line == 0, dest.astype(F32), 0.0)
    meta = jnp.where(line == 1, within, meta)
    meta = jnp.where(line == 2, label.astype(F32), meta)
    outgoing[row_count:, :] = meta.astype(BF16)

    loads[4].wait()
    loads[5].wait()
    cells = frames.shape[0]
    frame = cells // frame_count
    hidden[...] = dot(frames[...], conv[0])
    hidden[frame:, :] += dot(frames[: cells - frame, :], conv[1])
    hidden[2 * frame :, :] += dot(frames[: cells - 2 * frame, :], conv[2])
    value = hidden[...]
    active = (value * jax.nn.sigmoid(value)).astype(BF16)
    loads[6].wait()
    channels = lat_ref.shape[0]
    per = latent // channels
    narrow = dot_nt(active, lat_ref[...]).astype(BF16)
    lane = iota((channels, LANES), 1)
    spread = ((lane % channels == iota((channels, LANES), 0)) & (lane < latent)).astype(F32)
    wide = dot(narrow, spread.astype(BF16))
    wide = jnp.where(
        iota((cells, LANES), 1) // channels == iota((cells, LANES), 0) % per, wide, 0.0
    ).astype(BF16)
    gather = (iota((row_count, cells), 1) // per == iota((row_count, cells), 0)).astype(F32)
    patches = dot(gather.astype(BF16), wide)
    narrow_patches = patches[:, :latent].astype(BF16)

    def norm_part(k, square):
        x = dot(narrow_patches, embed[:, pl.ds(pl.multiple_of(k * tile, tile), tile)])
        x = x * x
        for i in range(tile // LANES):
            square = square + x[:, i * LANES : (i + 1) * LANES]
        return square

    square = lax.fori_loop(0, depth // tile, norm_part, jnp.zeros((row_count, LANES), F32))
    scale = lax.rsqrt(jnp.sum(square, axis=1, keepdims=True) / depth + EPS)
    high = scale.astype(BF16).astype(F32)
    middle = (scale - high).astype(BF16).astype(F32)
    low = scale - high - middle
    lane = iota((row_count, LANES), 1)
    line = iota((row_count, LANES), 0)
    placed = jnp.where(line == latent + 3, label, 0).astype(F32).astype(BF16)
    message = patches + dot_nt((line == lane).astype(F32).astype(BF16), placed)
    message = jnp.where(lane == latent, high, message)
    message = jnp.where(lane == latent + 1, middle, message)
    message = jnp.where(lane == latent + 2, low, message)
    outgoing[:row_count, :] = message.astype(BF16)

    pl.semaphore_wait(barrier, shards)
    sends = []
    for d in range(shards):
        send = pltpu.make_async_remote_copy(
            src_ref=outgoing, dst_ref=rows_out.at[ctx],
            send_sem=row_send.at[d], recv_sem=row_recv.at[d],
            device_id={"section": other, "ctx": lax.rem(ctx + d, shards)}, device_id_type=MESH,
        )
        send.start()
        sends.append(send)

    def swap(j):
        return pltpu.make_async_remote_copy(
            src_ref=mine.at[j], dst_ref=weff_out.at[section, j],
            send_sem=half_send.at[j], recv_sem=half_recv.at[j],
            device_id={"section": other}, device_id_type=MESH,
        )

    def keep(j):
        return pltpu.make_async_copy(mine.at[j], weff_out.at[section, j], keep_sem.at[j])

    def contract(j, carry):
        total[...] = jnp.zeros_like(total)

        def piece(p, inner):
            stream(j, p).wait()
            part = pl.ds(pl.multiple_of(p * step, step), step)
            total[...] += dot(scaled[:, part], qkv[j, part, :])
            return inner

        lax.fori_loop(0, pieces, piece, 0)
        full = total[...]
        if split:
            full = full[:latent] + full[latent:]
        mine[j] = full.astype(BF16)
        swap(j).start()
        keep(j).start()
        return carry

    lax.fori_loop(0, 3, contract, 0)
    for send in sends:
        send.wait()
    for j in range(3):
        keep(j).wait()
        swap(j).wait()


def attend_kernel(
    shards, capacity, rows_ref, weff_ref, out_ref,
    picked_ref, picked_floor, barred, rows, scales, floors, tags, keys_ref, values_ref,
):
    ctx = lax.axis_index("ctx").astype(F32)
    row_count = rows_ref.shape[1] - META
    latent, width = weff_ref.shape[2:]
    slots = out_ref.shape[0]

    @pl.when(pl.program_id(0) == 0)
    def _():
        def constants(block):
            scale = (
                block[:, latent : latent + 1].astype(F32)
                + block[:, latent + 1 : latent + 2].astype(F32)
                + block[:, latent + 2 : latent + 3].astype(F32)
            )
            return scale, block[:, latent + 3 : latent + 4].astype(F32).astype(jnp.int32)

        lane = iota((row_count, LANES), 1)
        picked = jnp.zeros((slots, LANES), F32)
        for source in range(shards):
            meta = rows_ref[source, row_count:, :].astype(F32)
            spot = jnp.where(meta[0:1, :] == ctx, meta[1:2, :] + source * capacity, -1.0)
            block = rows_ref[source, :row_count, :]
            taken = spot.astype(jnp.int32) == iota((slots, row_count), 0)
            picked = picked + dot(taken.astype(F32).astype(BF16), block)
            scale, tag = constants(block)
            part = slice(source * row_count, (source + 1) * row_count)
            rows[part, :] = block
            scales[part, :] = jnp.broadcast_to(scale, (row_count, LANES))
            floors[part, :] = jnp.broadcast_to(HEAD * EPS / (scale * scale), (row_count, LANES))
            tags[part, :] = (lane == tag).astype(F32).astype(BF16)
        picked = picked.astype(BF16)
        picked_ref[...] = picked
        scale, tag = constants(picked)
        scale = jnp.where(tag > 0, scale, 1.0)
        picked_floor[...] = jnp.broadcast_to(HEAD * EPS / (scale * scale), (slots, LANES))
        same = (iota((slots, LANES), 1) == tag) & (tag > 0)
        barred[...] = jnp.where(same, 0.0, -BARRED).astype(BF16)

    square_sum = (iota((width, width), 0) // HEAD == iota((width, width), 1) // HEAD)
    square_sum = square_sum.astype(F32).astype(BF16)
    ones = jnp.ones((rows.shape[0], HEAD), BF16)
    gain_q = HEAD**0.5 * LOG2E
    heads = [slice(h * HEAD, (h + 1) * HEAD) for h in range(width // HEAD)]

    for source in range(shards):
        part = slice(source * row_count, (source + 1) * row_count)
        block = rows[part, :latent]
        k = dot(block, weff_ref[0, 1])
        v = dot(block, weff_ref[0, 2])
        power = dot((k * k).astype(BF16), square_sum)
        for head in heads:
            keys_ref[part, head] = (k[:, head] * lax.rsqrt(power[:, head] + floors[part, :])).astype(BF16)
            values_ref[part, head] = (v[:, head] * scales[part, :]).astype(BF16)
    q = dot(picked_ref[:, :latent], weff_ref[0, 0])
    power = dot((q * q).astype(BF16), square_sum)
    for head in heads:
        scale = lax.rsqrt(power[:, head] + picked_floor[...]) * gain_q
        queries = (q[:, head] * scale).astype(BF16)
        scores = dot_nt(
            jnp.concatenate([queries, barred[...]], axis=1),
            jnp.concatenate([keys_ref[:, head], tags[...]], axis=1),
        )
        weights = jnp.exp2(scores).astype(BF16)
        both = dot(weights, jnp.concatenate([values_ref[:, head], ones], axis=1))
        den = both[:, HEAD:]
        out_ref[:, head] = (both[:, :HEAD] / jnp.where(den > 0.0, den, 1.0)).astype(BF16)


def on_device(shards, sections, frames, w_conv, w_lat, dest, pick, w_embed, gain, w_qkv):
    _, frame_count, frame, channels = frames.shape
    latent, depth = w_embed.shape
    cells = frame_count * frame
    row_count = dest.shape[1]
    columns = w_qkv.shape[2]
    half = columns // sections
    pieces = 4
    split = SPLIT
    capacity = max(2, 3 * row_count // (2 * shards))
    slots = shards * capacity
    total_rows = shards * row_count
    width = min(half, 2 * HEAD)
    groups = half // width
    rows, weff = pl.pallas_call(
        functools.partial(encode_kernel, shards, frame_count, pieces, split),
        out_shape=(
            jax.ShapeDtypeStruct((shards, row_count + META, LANES), BF16),
            jax.ShapeDtypeStruct((sections, 3, latent, half), BF16),
        ),
        in_specs=[HBM] * 8,
        out_specs=(HBM, HBM),
        scratch_shapes=[
            pltpu.VMEM((cells, channels), BF16),
            pltpu.VMEM(w_conv.shape, BF16),
            pltpu.VMEM((w_lat.shape[1], channels), BF16),
            pltpu.VMEM((sections, 1, row_count), jnp.int32),
            pltpu.VMEM((sections, row_count), jnp.int32),
            pltpu.VMEM((latent, depth), BF16),
            pltpu.VMEM((1, depth), F32),
            pltpu.VMEM((3, depth, half), BF16),
            pltpu.VMEM((2 * latent if split else latent, depth), BF16),
            pltpu.VMEM((cells, channels), F32),
            pltpu.VMEM((row_count + META, LANES), BF16),
            pltpu.VMEM((3, latent, half), BF16),
            pltpu.VMEM((2 * latent if split else latent, half), F32),
            pltpu.SemaphoreType.DMA((7,)),
            pltpu.SemaphoreType.DMA((3 * pieces,)),
            pltpu.SemaphoreType.DMA((shards,)),
            pltpu.SemaphoreType.DMA((shards,)),
            pltpu.SemaphoreType.DMA((3,)),
            pltpu.SemaphoreType.DMA((3,)),
            pltpu.SemaphoreType.DMA((3,)),
        ],
        compiler_params=pltpu.CompilerParams(
            collective_id=0, has_side_effects=True, vmem_limit_bytes=67043328
        ),
    )(
        frames.reshape(cells, channels),
        w_conv,
        w_lat.T,
        dest.transpose(0, 2, 1),
        pick,
        w_embed,
        gain.reshape(1, depth),
        w_qkv.transpose(1, 0, 2),
    )
    out = pl.pallas_call(
        functools.partial(attend_kernel, shards, capacity),
        grid=(sections * groups,),
        out_shape=jax.ShapeDtypeStruct((slots, columns), BF16),
        in_specs=[
            pl.BlockSpec((shards, row_count + META, LANES), lambda i: (0, 0, 0)),
            pl.BlockSpec((1, 3, latent, width), lambda i: (i // groups, 0, 0, i % groups)),
        ],
        out_specs=pl.BlockSpec((slots, width), lambda i: (0, i)),
        scratch_shapes=[
            pltpu.VMEM((slots, LANES), BF16),
            pltpu.VMEM((slots, LANES), F32),
            pltpu.VMEM((slots, LANES), BF16),
            pltpu.VMEM((total_rows, LANES), BF16),
            pltpu.VMEM((total_rows, LANES), F32),
            pltpu.VMEM((total_rows, LANES), F32),
            pltpu.VMEM((total_rows, LANES), BF16),
            pltpu.VMEM((total_rows, width), BF16),
            pltpu.VMEM((total_rows, width), BF16),
        ],
        compiler_params=pltpu.CompilerParams(vmem_limit_bytes=67043328),
    )(rows, weff)
    return out.reshape(1, slots, columns)


def solution(mesh):
    in_specs = (
        P("section", "ctx", None, None),
        P(),
        P(),
        P(None, "ctx", None),
        P(None, "ctx"),
        P(),
        P(),
        P(None, None, "mp"),
    )
    return jax.shard_map(
        functools.partial(on_device, mesh.shape["ctx"], mesh.shape["section"]),
        mesh=mesh,
        in_specs=in_specs,
        out_specs=P("section", "ctx", "mp"),
        check_vma=False,
    )
```

time: 21.7 us -> 24.6 us (1.13)
  the two profiles are of different devices: /device:TPU:0 before, /device:TPU:1 now
where the time goes in v3:
time: 24.6 us; the launch traced here: 24.4 us
  Pallas kernels  24.4 us (99%)
    pallas_call x1, Pallas kernels, on_device(): pl.pallas_call(functools.partial(encode_kernel, shards, frame_count, piec...  17.2 us
    pallas_call x1, Pallas kernels, on_device(): pl.pallas_call(functools.partial(attend_kernel, shards, capacity), grid=(...  7.2 us

profile of v3, /device:TPU:1, one launch (start us, length us, event | category | flops | bytes accessed | tf_op | source)
XLA Modules:
  0.0 24.4 jit_solution(9522412691735957122)
XLA Ops:
  0.0 17.2 %shard_map.82 = (bf16[4,144,128]{2,1,0:T(8,128)(2,1)}, bf16[2,3,64,512]{3,2,1,0:T(8,128)(2,1)}) custom-call(bf16[512,512]{1,0:T(8,128)(2,1)} %bitcast.7, bf16[3,512,512]{2,1,0:T(8,128)(2,1)} %conv_hbm.1, bf16[16,512]{1,0:T(8,128)(2,1)} %bitcast.9, s32[2,1,128]{2,1,0:T(1,128)} %bitcast.10, s32[2,128]{1,0:T(2,128)} %pick_hbm.1, bf16[64,6144]{1,0:T(8,128)(2,1)} %embed_hbm.1, ...), custom_call_target="tpu_custom_call" | custom-call | tf_op jit(solution)/shard_map/pallas_call | solution.py:290
  17.2 7.2 %shard_map.83 = bf16[192,1024]{1,0:T(8,128)(2,1)} custom-call(bf16[4,144,128]{2,1,0:T(8,128)(2,1)} %get-tuple-element.7.rows_ref, bf16[2,3,64,512]{3,2,1,0:T(8,128)(2,1)} %get-tuple-element.8.weff_ref), custom_call_target="tpu_custom_call" | custom-call | tf_op jit(solution)/shard_map/pallas_call | solution.py:333

commit v4 on v1

--- a/solution.py
+++ b/solution.py
@@ -12,11 +12,11 @@
 LANES = 128
 META = 16
 EPS = 1e-06
+SPLIT = True
 MESH = pl.DeviceIdType.MESH
 F32 = jnp.float32
 BF16 = jnp.bfloat16
-ANY = pl.BlockSpec(memory_space=pl.ANY)
-VMEM = pl.BlockSpec(memory_space=pltpu.VMEM)
+HBM = pl.BlockSpec(memory_space=pltpu.HBM)
 
 
 def dot(a, b):
@@ -32,10 +32,10 @@
 
 
 def encode_kernel(
-    shards, frame_count, pieces,
-    frames_hbm, conv_hbm, lat_ref, dest_ref, pick_ref, embed_hbm, gain_ref, qkv_hbm,
+    shards, frame_count, pieces, split,
+    frames_hbm, conv_hbm, lat_hbm, dest_hbm, pick_hbm, embed_hbm, gain_hbm, qkv_hbm,
     rows_out, weff_out,
-    frames, conv, embed, qkv, scaled, hidden, outgoing, mine,
+    frames, conv, lat_ref, dest_ref, pick_ref, embed, gain_ref, qkv, scaled, hidden, outgoing, mine, total,
     in_sem, qkv_sem, row_send, row_recv, half_send, half_recv, keep_sem,
 ):
     section = lax.axis_index("section")
@@ -48,22 +48,22 @@
     row_count = outgoing.shape[0] - META
 
     loads = [
-        pltpu.make_async_copy(frames_hbm, frames, in_sem.at[0]),
-        pltpu.make_async_copy(conv_hbm, conv, in_sem.at[1]),
-        pltpu.make_async_copy(embed_hbm, embed, in_sem.at[2]),
+        pltpu.make_async_copy(source, target, in_sem.at[i])
+        for i, (source, target) in enumerate((
+            (embed_hbm, embed), (gain_hbm, gain_ref), (dest_hbm, dest_ref), (pick_hbm, pick_ref),
+            (frames_hbm, frames), (conv_hbm, conv), (lat_hbm, lat_ref),
+        ))
     ]
     for load in loads:
         load.start()
     columns = pl.ds(pl.multiple_of(section * half, LANES), half)
-    streams = []
-    for j in range(3):
-        for p in range(pieces):
-            part = pl.ds(p * step, step)
-            stream = pltpu.make_async_copy(
-                qkv_hbm.at[j, part, columns], qkv.at[j, part, :], qkv_sem.at[j * pieces + p]
-            )
-            stream.start()
-            streams.append(stream)
+
+    def stream(j, p):
+        part = pl.ds(pl.multiple_of(p * step, step), step)
+        return pltpu.make_async_copy(
+            qkv_hbm.at[j, part, columns], qkv.at[j, part, :], qkv_sem.at[j * pieces + p]
+        )
+
 
     barrier = pltpu.get_barrier_semaphore()
     for d in range(shards):
@@ -72,6 +72,26 @@
             device_id={"section": other, "ctx": lax.rem(ctx + d, shards)}, device_id_type=MESH,
         )
 
+    loads[0].wait()
+    loads[1].wait()
+    tile = 512
+
+    def scale_part(k, carry):
+        part = pl.ds(pl.multiple_of(k * tile, tile), tile)
+        full = embed[:, part].astype(F32) * gain_ref[:, part]
+        top = full.astype(BF16)
+        scaled[:latent, part] = top
+        if split:
+            scaled[latent:, part] = (full - top.astype(F32)).astype(BF16)
+        return carry
+
+    lax.fori_loop(0, depth // tile, scale_part, 0)
+
+    for load in loads[2:]:
+        load.wait()
+    for j in range(3):
+        for p in range(pieces):
+            stream(j, p).start()
     first = section == 0
     dest = jnp.where(first, dest_ref[0], dest_ref[1])
     pick = jnp.where(first, pick_ref[0:1, :], pick_ref[1:2, :])
@@ -88,8 +108,6 @@
     meta = jnp.where(line == 2, label.astype(F32), meta)
     outgoing[row_count:, :] = meta.astype(BF16)
 
-    loads[0].wait()
-    loads[1].wait()
     cells = frames.shape[0]
     frame = cells // frame_count
     hidden[...] = dot(frames[...], conv[0])
@@ -108,21 +126,25 @@
     ).astype(BF16)
     gather = (iota((row_count, cells), 1) // per == iota((row_count, cells), 0)).astype(F32)
     patches = dot(gather.astype(BF16), wide)
-    loads[2].wait()
     narrow_patches = patches[:, :latent].astype(BF16)
-    square = jnp.zeros((row_count, LANES), F32)
-    tile = 512
-    for k in range(depth // tile):
-        x = dot(narrow_patches, embed[:, k * tile : (k + 1) * tile])
+
+    def norm_part(k, square):
+        x = dot(narrow_patches, embed[:, pl.ds(pl.multiple_of(k * tile, tile), tile)])
         x = x * x
         for i in range(tile // LANES):
             square = square + x[:, i * LANES : (i + 1) * LANES]
+        return square
+
+    square = lax.fori_loop(0, depth // tile, norm_part, jnp.zeros((row_count, LANES), F32))
     scale = lax.rsqrt(jnp.sum(square, axis=1, keepdims=True) / depth + EPS)
     high = scale.astype(BF16).astype(F32)
     middle = (scale - high).astype(BF16).astype(F32)
     low = scale - high - middle
     lane = iota((row_count, LANES), 1)
-    message = jnp.where(lane == latent, high, patches)
+    line = iota((row_count, LANES), 0)
+    placed = jnp.where(line == latent + 3, label, 0).astype(F32).astype(BF16)
+    message = patches + dot_nt((line == lane).astype(F32).astype(BF16), placed)
+    message = jnp.where(lane == latent, high, message)
     message = jnp.where(lane == latent + 1, middle, message)
     message = jnp.where(lane == latent + 2, low, message)
     outgoing[:row_count, :] = message.astype(BF16)
@@ -138,35 +160,40 @@
         send.start()
         sends.append(send)
 
-    for k in range(depth // tile):
-        part = slice(k * tile, (k + 1) * tile)
-        full = embed[:, part].astype(F32) * gain_ref[:, part]
-        top = full.astype(BF16)
-        scaled[:latent, part] = top
-        scaled[latent:, part] = (full - top.astype(F32)).astype(BF16)
-
-    keeps = []
-    for j in range(3):
-        total = jnp.zeros((2 * latent, half), F32)
-        for p in range(pieces):
-            streams[j * pieces + p].wait()
-            part = slice(p * step, (p + 1) * step)
-            total = total + dot(scaled[:, part], qkv[j, part, :])
-        mine[j] = (total[:latent] + total[latent:]).astype(BF16)
-        send = pltpu.make_async_remote_copy(
+    def swap(j):
+        return pltpu.make_async_remote_copy(
             src_ref=mine.at[j], dst_ref=weff_out.at[section, j],
             send_sem=half_send.at[j], recv_sem=half_recv.at[j],
             device_id={"section": other}, device_id_type=MESH,
         )
-        send.start()
-        sends.append(send)
-        keep = pltpu.make_async_copy(mine.at[j], weff_out.at[section, j], keep_sem.at[j])
-        keep.start()
-        keeps.append(keep)
-    for keep in keeps:
-        keep.wait()
+
+    def keep(j):
+        return pltpu.make_async_copy(mine.at[j], weff_out.at[section, j], keep_sem.at[j])
+
+    def contract(j, carry):
+        total[...] = jnp.zeros_like(total)
+
+        def piece(p, inner):
+            stream(j, p).wait()
+            part = pl.ds(pl.multiple_of(p * step, step), step)
+            total[...] += dot(scaled[:, part], qkv[j, part, :])
+            return inner
+
+        lax.fori_loop(0, pieces, piece, 0)
+        full = total[...]
+        if split:
+            full = full[:latent] + full[latent:]
+        mine[j] = full.astype(BF16)
+        swap(j).start()
+        keep(j).start()
+        return carry
+
+    lax.fori_loop(0, 3, contract, 0)
     for send in sends:
         send.wait()
+    for j in range(3):
+        keep(j).wait()
+        swap(j).wait()
 
 
 def attend_kernel(shards, capacity, rows_ref, weff_ref, out_ref, picked_ref, row_ref, mask_ref):
@@ -232,26 +259,32 @@
     columns = w_qkv.shape[2]
     half = columns // sections
     pieces = 4
+    split = SPLIT
     capacity = max(2, 3 * row_count // (2 * shards))
     slots = shards * capacity
     rows, weff = pl.pallas_call(
-        functools.partial(encode_kernel, shards, frame_count, pieces),
+        functools.partial(encode_kernel, shards, frame_count, pieces, split),
         out_shape=(
             jax.ShapeDtypeStruct((shards, row_count + META, LANES), BF16),
             jax.ShapeDtypeStruct((sections, 3, latent, half), BF16),
         ),
-        in_specs=[ANY, ANY, VMEM, VMEM, VMEM, ANY, VMEM, ANY],
-        out_specs=(ANY, ANY),
+        in_specs=[HBM] * 8,
+        out_specs=(HBM, HBM),
         scratch_shapes=[
             pltpu.VMEM((cells, channels), BF16),
             pltpu.VMEM(w_conv.shape, BF16),
+            pltpu.VMEM((w_lat.shape[1], channels), BF16),
+            pltpu.VMEM((sections, 1, row_count), jnp.int32),
+            pltpu.VMEM((sections, row_count), jnp.int32),
             pltpu.VMEM((latent, depth), BF16),
+            pltpu.VMEM((1, depth), F32),
             pltpu.VMEM((3, depth, half), BF16),
-            pltpu.VMEM((2 * latent, depth), BF16),
+            pltpu.VMEM((2 * latent if split else latent, depth), BF16),
             pltpu.VMEM((cells, channels), F32),
             pltpu.VMEM((row_count + META, LANES), BF16),
             pltpu.VMEM((3, latent, half), BF16),
-            pltpu.SemaphoreType.DMA((3,)),
+            pltpu.VMEM((2 * latent if split else latent, half), F32),
+            pltpu.SemaphoreType.DMA((7,)),
             pltpu.SemaphoreType.DMA((3 * pieces,)),
             pltpu.SemaphoreType.DMA((shards,)),
             pltpu.SemaphoreType.DMA((shards,)),
@@ -260,7 +293,7 @@
             pltpu.SemaphoreType.DMA((3,)),
         ],
         compiler_params=pltpu.CompilerParams(
-            collective_id=0, has_side_effects=True, vmem_limit_bytes=48 << 20
+            collective_id=0, has_side_effects=True, vmem_limit_bytes=67043328
         ),
     )(
         frames.reshape(cells, channels),
@@ -286,7 +319,7 @@
             pltpu.VMEM((shards * row_count, LANES), BF16),
             pltpu.VMEM((slots, shards * row_count), F32),
         ],
-        compiler_params=pltpu.CompilerParams(vmem_limit_bytes=48 << 20),
+        compiler_params=pltpu.CompilerParams(vmem_limit_bytes=67043328),
     )(rows, weff)
     return out.reshape(1, slots, columns)
 

time: 21.7 us -> 17.9 us (0.82)
  the two profiles are of different devices: /device:TPU:0 before, /device:TPU:1 now
where the time goes in v4:
time: 17.9 us; the launch traced here: 17.8 us
  Pallas kernels  17.7 us (99%)
    pallas_call x1, Pallas kernels, on_device(): pl.pallas_call(functools.partial(encode_kernel, shards, frame_count, piec...  12.4 us
    pallas_call x1, Pallas kernels, on_device(): pl.pallas_call(functools.partial(attend_kernel, shards, capacity), grid=(...  5.33 us

profile of v4, /device:TPU:1, one launch (start us, length us, event | category | flops | bytes accessed | tf_op | source)
XLA Modules:
  0.0 17.8 jit_solution(16857916862454730403)
XLA Ops:
  0.0 12.4 %shard_map.82 = (bf16[4,144,128]{2,1,0:T(8,128)(2,1)}, bf16[2,3,64,512]{3,2,1,0:T(8,128)(2,1)}) custom-call(bf16[512,512]{1,0:T(8,128)(2,1)} %bitcast.7, bf16[3,512,512]{2,1,0:T(8,128)(2,1)} %conv_hbm.1, bf16[16,512]{1,0:T(8,128)(2,1)} %bitcast.9, s32[2,1,128]{2,1,0:T(1,128)} %bitcast.10, s32[2,128]{1,0:T(2,128)} %pick_hbm.1, bf16[64,6144]{1,0:T(8,128)(2,1)} %embed_hbm.1, ...), custom_call_target="tpu_custom_call" | custom-call | tf_op jit(solution)/shard_map/pallas_call | solution.py:265
  12.4 5.3 %shard_map.83 = bf16[192,1024]{1,0:T(8,128)(2,1)} custom-call(bf16[4,144,128]{2,1,0:T(8,128)(2,1)} %get-tuple-element.7.rows_ref, bf16[2,3,64,512]{3,2,1,0:T(8,128)(2,1)} %get-tuple-element.8.weff_ref), custom_call_target="tpu_custom_call" | custom-call | tf_op jit(solution)/shard_map/pallas_call | solution.py:308

commit v5 on v4

--- a/solution.py
+++ b/solution.py
@@ -12,7 +12,7 @@
 LANES = 128
 META = 16
 EPS = 1e-06
-SPLIT = True
+SPLIT = False
 MESH = pl.DeviceIdType.MESH
 F32 = jnp.float32
 BF16 = jnp.bfloat16

time: 17.9 us -> 17.9 us (level)
  no operation moved by 1% of the time
where the time goes in v5:
time: 17.9 us; the launch traced here: 17.8 us
  Pallas kernels  17.7 us (99%)
    pallas_call x1, Pallas kernels, on_device(): pl.pallas_call(functools.partial(encode_kernel, shards, frame_count, piec...  12.4 us
    pallas_call x1, Pallas kernels, on_device(): pl.pallas_call(functools.partial(attend_kernel, shards, capacity), grid=(...  5.33 us

profile of v5, /device:TPU:1, one launch (start us, length us, event | category | flops | bytes accessed | tf_op | source)
XLA Modules:
  0.0 17.8 jit_solution(17480343490032779232)
XLA Ops:
  0.0 12.4 %shard_map.82 = (bf16[4,144,128]{2,1,0:T(8,128)(2,1)}, bf16[2,3,64,512]{3,2,1,0:T(8,128)(2,1)}) custom-call(bf16[512,512]{1,0:T(8,128)(2,1)} %bitcast.7, bf16[3,512,512]{2,1,0:T(8,128)(2,1)} %conv_hbm.1, bf16[16,512]{1,0:T(8,128)(2,1)} %bitcast.9, s32[2,1,128]{2,1,0:T(1,128)} %bitcast.10, s32[2,128]{1,0:T(2,128)} %pick_hbm.1, bf16[64,6144]{1,0:T(8,128)(2,1)} %embed_hbm.1, ...), custom_call_target="tpu_custom_call" | custom-call | tf_op jit(solution)/shard_map/pallas_call | solution.py:265
  12.4 5.3 %shard_map.83 = bf16[192,1024]{1,0:T(8,128)(2,1)} custom-call(bf16[4,144,128]{2,1,0:T(8,128)(2,1)} %get-tuple-element.7.rows_ref, bf16[2,3,64,512]{3,2,1,0:T(8,128)(2,1)} %get-tuple-element.8.weff_ref), custom_call_target="tpu_custom_call" | custom-call | tf_op jit(solution)/shard_map/pallas_call | solution.py:308
